TPU v7x, 512 devices: a whole 4x8x8 slice. The times are simulated.
512 devices in a mesh: row: 16 (over x, z_lo), col: 32 (over y, z_hi, core).
Axes of the slice: x: 4, y: 8, z: 8 (z_hi: 2, z_lo: 4; z = z_hi * 4 + z_lo), core: 2. Of those that a mesh axis runs over, the one named last changes fastest.
Arguments:
- covariance: float32 [16384, 16384], P('row', 'col'), may hold values from -7 to 14, as said below
- wind_mask: int32 [2, 16384], replicated, may hold values 0 or 1
- wind_speed: float32 [2, 16384], replicated, may hold values from 0.02 to 0.3
- obs_cells: int32 [256, 128], replicated, may hold values from 0 to 16383
- obs_scale: float32 [256], replicated, may hold values from 0.05 to 0.2
- gain: bfloat16 [16384, 256], P('row'), may hold values from -0.375 to 0.375
Outputs:
- updated: float32 [16384, 16384], P('row', 'col')
Inputs may be any that keep to these rules, and one draw needn't show every extreme that they name: A covariance window.
All inputs are finite; a program needn't handle non-finite values.
Results may differ from a plain program's by a relative error of at most 0.0003.
Values sent between devices are 32-bit elements; how exact they have to be, the bound alone decides.
No kernel may reach another device: no remote copies, remote signals or barrier semaphores. Data moves between devices by JAX's collectives and lax.ppermute only.
A program may use at most 64 MiB of HBM per device.

v0:
```python
import jax
import jax.numpy as jnp
from jax import lax
from jax.sharding import PartitionSpec as P

MAPX = 256
diffusion = 0.05


def extended_2(cells, sides, width):
    for axis, dim in sides:
        count = lax.axis_size(axis)
        ends = count - 1
        head = lax.slice_in_dim(cells, 0, width, axis=dim)
        tail = lax.slice_in_dim(cells, cells.shape[dim] - width, cells.shape[dim], axis=dim)
        cells = jnp.concatenate(
            [
                lax.ppermute(tail, axis, [(i, (i + 1) % count) for i in range(ends)]),
                cells,
                lax.ppermute(head, axis, [((i + 1) % count, i) for i in range(ends)]),
            ],
            axis=dim,
        )
    return cells


def coefficients(wind_mask, wind_speed):
    cell_total = wind_speed.shape[1]
    cells = jnp.arange(cell_total, dtype=jnp.int32)
    map_column = cells % MAPX
    map_row = cells // MAPX
    last_row = cell_total // MAPX - 1
    speed_x = wind_speed[0]
    speed_y = wind_speed[1]
    sign_x = wind_mask[0].astype(jnp.float32)
    sign_y = wind_mask[1].astype(jnp.float32)
    middle = 1.0 - speed_x - speed_y - 4.0 * diffusion
    western = jnp.where(map_column > 0, speed_x * sign_x + diffusion, 0.0)
    eastern = jnp.where(map_column < MAPX - 1, speed_x * (1.0 - sign_x) + diffusion, 0.0)
    northern = jnp.where(map_row > 0, speed_y * sign_y + diffusion, 0.0)
    southern = jnp.where(map_row < last_row, speed_y * (1.0 - sign_y) + diffusion, 0.0)
    return jnp.stack([middle, western, eastern, northern, southern])


def transport(extended, coef, along_dim):
    length = extended.shape[along_dim] - 2 * MAPX
    if along_dim == 0:
        weights = coef[:, :, None]
    else:
        weights = coef[:, None, :]

    def window_at(offset):
        return lax.slice_in_dim(extended, offset, offset + length, axis=along_dim)

    result = weights[0] * window_at(MAPX) + weights[1] * window_at(MAPX - 1)
    result = result + weights[2] * window_at(MAPX + 1)
    result = result + weights[3] * window_at(0) + weights[4] * window_at(2 * MAPX)
    return result


def local(covariance, wind_mask, wind_speed, obs_cells, obs_scale, gain):
    row_count, col_count = covariance.shape
    table = coefficients(wind_mask, wind_speed)
    row_start = lax.axis_index("row") * row_count
    col_start = lax.axis_index("col") * col_count
    row_coef = lax.dynamic_slice_in_dim(table, row_start, row_count, 1)
    col_coef = lax.dynamic_slice_in_dim(table, col_start, col_count, 1)
    moved_field = covariance
    for repeat in range(2):
        extended = extended_2(moved_field, (("row", 0),), MAPX)
        moved_field = transport(extended, row_coef, 0)
        extended = extended_2(moved_field, (("col", 1),), MAPX)
        moved_field = transport(extended, col_coef, 1)
    obs_count, foot_count = obs_cells.shape
    obs_block = 16
    local_cell = (obs_cells - row_start).reshape(obs_count // obs_block, obs_block, foot_count)
    row_ids = jnp.arange(row_count, dtype=jnp.int32)

    def count_block(cell_block):
        hits = (cell_block[:, :, None] == row_ids[None, None, :]).astype(jnp.float32)
        return jnp.sum(hits, axis=1)

    counts = lax.map(count_block, local_cell).reshape(obs_count, row_count)
    select = counts * obs_scale[:, None]
    part_sum = jnp.dot(
        select, moved_field, precision=lax.Precision.HIGHEST, preferred_element_type=jnp.float32
    )
    gain_panel = gain.astype(jnp.float32)
    observed = lax.psum(part_sum, "row")
    update = jnp.dot(
        gain_panel, observed, precision=lax.Precision.HIGHEST, preferred_element_type=jnp.float32
    )
    return moved_field - update


def solution(mesh):
    placed = (P("row", "col"), P(), P(), P(), P(), P("row", None))
    return jax.shard_map(
        local, mesh=mesh, in_specs=placed, out_specs=P("row", "col"), check_vma=False
    )
```

profile of v0, /device:TPU:8, one launch (start us, length us, event | category | flops | bytes accessed | tf_op | source)
XLA Modules:
  0.0 402.4 jit_solution(15827598846107994043)
XLA Ops:
  6.5 2.0 copy.13
  9.6 5.1 %collective-permute-start = (f32[256,512]{0,1:T(8,128)}, f32[256,512]{0,1:T(8,128)}, u32[]{:S(2)}, u32[]{:S(2)}) collective-permute-start(f32[256,512]{0,1:T(8,128)} %get-tuple-element.48), channel_id=1, source_target_pairs={{0,32},{32,64},{64,96},{96,128},{128,160},{160,192},{192,224},{224... | collective-permute-start | bytes 1572872 | tf_op jit(solution)/shard_map/ppermute | solution.py:18
  17.1 8.3 %collective-permute-done = f32[256,512]{0,1:T(8,128)} collective-permute-done((f32[256,512]{0,1:T(8,128)}, f32[256,512]{0,1:T(8,128)}, u32[]{:S(2)}, u32[]{:S(2)}) %collective-permute-start) | collective-permute-done | bytes 524320 | tf_op jit(solution)/shard_map/ppermute | solution.py:18
  25.4 15.6 %collective-permute-done.1 = f32[256,512]{0,1:T(8,128)} collective-permute-done((f32[256,512]{0,1:T(8,128)}, f32[256,512]{0,1:T(8,128)}, u32[]{:S(2)}, u32[]{:S(2)}) %collective-permute-start.1) | collective-permute-done | bytes 524320 | tf_op jit(solution)/shard_map/ppermute | solution.py:20
  41.0 5.5 %fusion.14 = f32[1024,512]{0,1:T(8,128)S(1)} fusion(f32[1024,512]{0,1:T(8,128)} %copy-done.2, f32[256,512]{0,1:T(8,128)} %collective-permute-done.1, f32[256,512]{0,1:T(8,128)} %collective-permute-done, f32[1024]{0:T(1024)S(1)} %bitcast.36, f32[1024]{0:T(1024)S(1)} %bitcast.30, f32[1024]{0:T(1024)S(1)} %bitcast.32, f32[1024]{0:T(1024)S(1)} %bitcast.34, ...), kind=kLoop, calls=%fused_computation.33 | loop fusion | flops 6815744 | bytes 5263360 | tf_op jit(solution)/shard_map/add | solution.py:57
  46.4 1.5 fusion.44
  47.9 1.9 collective-permute-start.2
  49.8 8.9 %collective-permute-start.3 = (f32[1024,256]{0,1:T(8,128)}, f32[1024,256]{0,1:T(8,128)}, u32[]{:S(2)}, u32[]{:S(2)}) collective-permute-start(f32[1024,256]{0,1:T(8,128)} %get-tuple-element.47), channel_id=1, source_target_pairs={{1,0},{2,1},{3,2},{4,3},{5,4},{6,5},{7,6},{8,7},{9,8},{10,9},{11,1... | collective-permute-start | bytes 3145736 | tf_op jit(solution)/shard_map/ppermute | solution.py:20
  58.8 22.3 %collective-permute-done.2 = f32[1024,256]{0,1:T(8,128)} collective-permute-done((f32[1024,256]{0,1:T(8,128)}, f32[1024,256]{0,1:T(8,128)}, u32[]{:S(2)}, u32[]{:S(2)}) %collective-permute-start.2) | collective-permute-done | bytes 1048608 | tf_op jit(solution)/shard_map/ppermute | solution.py:18
  81.1 2.6 collective-permute-done.3
  83.7 3.3 fusion.30
  88.4 2.6 collective-permute-start.4
  92.3 12.9 %collective-permute-done.4 = f32[256,512]{0,1:T(8,128)S(1)} collective-permute-done((f32[256,512]{0,1:T(8,128)S(1)}, f32[256,512]{0,1:T(8,128)S(1)}, u32[]{:S(2)}, u32[]{:S(2)}) %collective-permute-start.4) | collective-permute-done | bytes 524320 | tf_op jit(solution)/shard_map/ppermute | solution.py:18
  105.2 10.1 %collective-permute-done.5 = f32[256,512]{0,1:T(8,128)} collective-permute-done((f32[256,512]{0,1:T(8,128)S(1)}, f32[256,512]{0,1:T(8,128)}, u32[]{:S(2)}, u32[]{:S(2)}) %collective-permute-start.5) | collective-permute-done | bytes 524320 | tf_op jit(solution)/shard_map/ppermute | solution.py:20
  115.3 5.2 %fusion.6 = f32[1024,512]{0,1:T(8,128)S(1)} fusion(f32[1024,512]{0,1:T(8,128)} %copy-done.3, f32[256,512]{0,1:T(8,128)} %collective-permute-done.5, f32[256,512]{0,1:T(8,128)S(1)} %collective-permute-done.4, f32[1024]{0:T(1024)S(1)} %bitcast.37, f32[1024]{0:T(1024)S(1)} %bitcast.31, f32[1024]{0:T(1024)S(1)} %bitcast.33, f32[1024]{0:T(1024)S(1)} %bitcast.35, ...), kind=kLoop, calls=%fused_computation.25 | loop fusion | flops 6815744 | bytes 5263360 | tf_op jit(solution)/shard_map/add | solution.py:57
  120.5 1.5 fusion.42
  121.9 17.8 %collective-permute-start.6 = (f32[1024,256]{0,1:T(8,128)}, f32[1024,256]{0,1:T(8,128)}, u32[]{:S(2)}, u32[]{:S(2)}) collective-permute-start(f32[1024,256]{0,1:T(8,128)} %get-tuple-element.42), channel_id=1, source_target_pairs={{0,1},{1,2},{2,3},{3,4},{4,5},{5,6},{6,7},{7,8},{8,9},{9,10},{10,1... | collective-permute-start | bytes 3145736 | tf_op jit(solution)/shard_map/ppermute | solution.py:18
  139.7 1.9 collective-permute-start.7
  141.7 32.9 %while.11 = (s32[]{:T(128)}, f32[16,16,1024]{2,1,0:T(8,128)}, s32[16,16,128]{2,1,0:T(8,128)S(1)}, s32[]{:T(128)}) while((s32[]{:T(128)}, f32[16,16,1024]{2,1,0:T(8,128)}, s32[16,16,128]{2,1,0:T(8,128)S(1)}, s32[]{:T(128)}) %tuple.42), condition=%wide.region_2.3_spmd.clone, body=%wide.region_0.2_spmd.clone.sunk | while | flops 6275074 | bytes 221753 | solution.py:83
  175.9 3.3 fusion.22
  180.6 2.7 fusion.46
  183.3 206.8 %all-reduce.2.cloned.1.call-done = f32[256,512]{1,0:T(8,128)} async-done(((f32[256,512]{1,0:T(8,128)}), f32[256,512]{1,0:T(8,128)}) %all-reduce.2.cloned.1.call-update) | async-done | bytes 524304 | tf_op jit(solution)/shard_map/psum | solution.py:89
  390.1 3.6 bitcast_subtract_fusion
  393.7 1.8 copy.18
  (79 shorter events, 41.6 us)
Async XLA Ops:
  6.5 383.5 %copy-start = (bf16[1024,256]{1,0:T(8,128)(2,1)S(1)}, bf16[1024,256]{1,0:T(8,128)(2,1)}, u32[]{:S(2)}) copy-start(bf16[1024,256]{1,0:T(8,128)(2,1)} %param.13) | copy-start | bytes 1572868
  6.5 383.5 %all-reduce.2.cloned.1.call-start = ((), (), s32[]{:S(2)}) async-start(), calls=%async_computation | async-start | bytes 1048576 | tf_op jit(solution)/shard_map/psum | solution.py:89
  8.5 32.4 %copy-start.2 = (f32[1024,512]{0,1:T(8,128)}, f32[1024,512]{0,1:T(8,128)S(1)}, u32[]{:S(2)}) copy-start(f32[1024,512]{0,1:T(8,128)S(1)} %copy.13) | copy-start | bytes 6291460
  8.5 7.5 %copy-start.5 = (s32[2,16384]{1,0:T(2,128)S(1)}, s32[2,16384]{1,0:T(2,128)}, u32[]{:S(2)}) copy-start(s32[2,16384]{1,0:T(2,128)} %param.9) | copy-start | bytes 393220
  8.5 7.5 %copy-start.6 = (f32[2,16384]{1,0:T(2,128)S(1)}, f32[2,16384]{1,0:T(2,128)}, u32[]{:S(2)}) copy-start(f32[2,16384]{1,0:T(2,128)} %param.10) | copy-start | bytes 393220
  9.6 15.8 %collective-permute-start = (f32[256,512]{0,1:T(8,128)}, f32[256,512]{0,1:T(8,128)}, u32[]{:S(2)}, u32[]{:S(2)}) collective-permute-start(f32[256,512]{0,1:T(8,128)} %get-tuple-element.48), channel_id=1, source_target_pairs={{0,32},{32,64},{64,96},{96,128},{128,160},{160,192},{192,224},{224... | collective-permute-start | bytes 1572872 | tf_op jit(solution)/shard_map/ppermute | solution.py:18
  14.7 26.3 %collective-permute-start.1 = (f32[256,512]{0,1:T(8,128)}, f32[256,512]{0,1:T(8,128)}, u32[]{:S(2)}, u32[]{:S(2)}) collective-permute-start(f32[256,512]{0,1:T(8,128)} %get-tuple-element.49), channel_id=1, source_target_pairs={{32,0},{64,32},{96,64},{128,96},{160,128},{192,160},{224,192},{256... | collective-permute-start | bytes 1572872 | tf_op jit(solution)/shard_map/ppermute | solution.py:20
  47.9 33.2 %collective-permute-start.2 = (f32[1024,256]{0,1:T(8,128)}, f32[1024,256]{0,1:T(8,128)}, u32[]{:S(2)}, u32[]{:S(2)}) collective-permute-start(f32[1024,256]{0,1:T(8,128)} %get-tuple-element.46), channel_id=1, source_target_pairs={{0,1},{1,2},{2,3},{3,4},{4,5},{5,6},{6,7},{7,8},{8,9},{9,10},{10,1... | collective-permute-start | bytes 3145736 | tf_op jit(solution)/shard_map/ppermute | solution.py:18
  49.8 33.9 %collective-permute-start.3 = (f32[1024,256]{0,1:T(8,128)}, f32[1024,256]{0,1:T(8,128)}, u32[]{:S(2)}, u32[]{:S(2)}) collective-permute-start(f32[1024,256]{0,1:T(8,128)} %get-tuple-element.47), channel_id=1, source_target_pairs={{1,0},{2,1},{3,2},{4,3},{5,4},{6,5},{7,6},{8,7},{9,8},{10,9},{11,1... | collective-permute-start | bytes 3145736 | tf_op jit(solution)/shard_map/ppermute | solution.py:20
  87.0 1.3 copy-start.3
  88.3 4.0 copy-start.4
  88.4 16.8 %collective-permute-start.4 = (f32[256,512]{0,1:T(8,128)S(1)}, f32[256,512]{0,1:T(8,128)S(1)}, u32[]{:S(2)}, u32[]{:S(2)}) collective-permute-start(f32[256,512]{0,1:T(8,128)S(1)} %get-tuple-element.44), channel_id=1, source_target_pairs={{0,32},{32,64},{64,96},{96,128},{128,160},{160,192},{192,224},{224... | collective-permute-start | bytes 1572872 | tf_op jit(solution)/shard_map/ppermute | solution.py:18
  91.0 24.3 %collective-permute-start.5 = (f32[256,512]{0,1:T(8,128)S(1)}, f32[256,512]{0,1:T(8,128)}, u32[]{:S(2)}, u32[]{:S(2)}) collective-permute-start(f32[256,512]{0,1:T(8,128)S(1)} %get-tuple-element.45), channel_id=1, source_target_pairs={{32,0},{64,32},{96,64},{128,96},{160,128},{192,160},{224,192},{256... | collective-permute-start | bytes 1572872 | tf_op jit(solution)/shard_map/ppermute | solution.py:20
  120.5 54.1 %copy-start.7 = (f32[256]{0:T(256)S(1)}, f32[256]{0:T(256)}, u32[]{:S(2)}) copy-start(f32[256]{0:T(256)} %param.12) | copy-start | bytes 3076
  121.9 54.0 %collective-permute-start.6 = (f32[1024,256]{0,1:T(8,128)}, f32[1024,256]{0,1:T(8,128)}, u32[]{:S(2)}, u32[]{:S(2)}) collective-permute-start(f32[1024,256]{0,1:T(8,128)} %get-tuple-element.42), channel_id=1, source_target_pairs={{0,1},{1,2},{2,3},{3,4},{4,5},{5,6},{6,7},{7,8},{8,9},{9,10},{10,1... | collective-permute-start | bytes 3145736 | tf_op jit(solution)/shard_map/ppermute | solution.py:18
  139.7 36.2 %collective-permute-start.7 = (f32[1024,256]{0,1:T(8,128)}, f32[1024,256]{0,1:T(8,128)}, u32[]{:S(2)}, u32[]{:S(2)}) collective-permute-start(f32[1024,256]{0,1:T(8,128)} %get-tuple-element.43), channel_id=1, source_target_pairs={{1,0},{2,1},{3,2},{4,3},{5,4},{6,5},{7,6},{8,7},{9,8},{10,9},{11,1... | collective-permute-start | bytes 3145736 | tf_op jit(solution)/shard_map/ppermute | solution.py:20
  179.2 1.3 copy-start.1
Sparse Core Ops, SparseCore 0:
  183.4 206.5 all-reduce.1
where the time goes:
time: 403 us; the launch traced here: 402 us
  waiting for transfers between devices  278 us (69%)
  other arithmetic  41.6 us (10%)
  starting transfers between devices  40.8 us (10%)
  local copies, waits for them, and re-layouts  21.4 us (5%)
  between operations  13.7 us (3%)
  matrix products  6.35 us (2%)
    psum x1, waiting for transfers between devices, local(): observed = lax.psum(part_sum, 'row')  207 us
    ppermute x4, waiting for transfers between devices, extended_2(): lax.ppermute(tail, axis, [(i, (i + 1) % count) for i in range(ends)])  43.4 us
    ppermute x4, waiting for transfers between devices, extended_2(): lax.ppermute(head, axis, [((i + 1) % count, i) for i in range(ends)])  28.3 us
    ppermute x4, starting transfers between devices, extended_2(): lax.ppermute(tail, axis, [(i, (i + 1) % count) for i in range(ends)])  27.4 us
    reduce_sum x16, other arithmetic, count_block(): return jnp.sum(hits, axis=1)  22.6 us
    add x4, other arithmetic, transport(): result + weights[3] * window_at(0) + weights[4] * window_at(2 * MAPX)  17.2 us
    ppermute x4, starting transfers between devices, extended_2(): lax.ppermute(head, axis, [((i + 1) % count, i) for i in range(ends)])  13.4 us
    dynamic_update_slice x16, local copies, waits for them, and re-layouts, local(): counts = lax.map(count_block, local_cell).reshape(obs_count, row_count)  10.1 us
  transfers between devices with their start and end apart: 9, of which 7 were waited for; matrix products, arithmetic and copies ran while one was open for 9% of the time, Pallas kernels for 0%

commit v1 on v0

--- a/solution.py
+++ b/solution.py
@@ -86,7 +86,7 @@
         select, moved_field, precision=lax.Precision.HIGHEST, preferred_element_type=jnp.float32
     )
     gain_panel = gain.astype(jnp.float32)
-    observed = lax.psum(part_sum, "row")
+    observed = jnp.sum(lax.all_gather(part_sum, "row"), axis=0)
     update = jnp.dot(
         gain_panel, observed, precision=lax.Precision.HIGHEST, preferred_element_type=jnp.float32
     )

time: 403 us -> 430 us (1.067)
  the two profiles are of different devices: /device:TPU:8 before, /device:TPU:1 now
where the time goes in v1:
time: 430 us; the launch traced here: 429 us
  waiting for transfers between devices  286 us (67%)
  starting transfers between devices  53.8 us (13%)
  other arithmetic  46.7 us (11%)
  local copies, waits for them, and re-layouts  22.6 us (5%)
  between operations  13.7 us (3%)
  matrix products  5.98 us (1%)
    all_gather x1, waiting for transfers between devices, local(): observed = jnp.sum(lax.all_gather(part_sum, 'row'), axis=0)  213 us
    ppermute x4, waiting for transfers between devices, extended_2(): lax.ppermute(tail, axis, [(i, (i + 1) % count) for i in range(ends)])  50.6 us
    ppermute x4, starting transfers between devices, extended_2(): lax.ppermute(tail, axis, [(i, (i + 1) % count) for i in range(ends)])  47.2 us
    ppermute x4, waiting for transfers between devices, extended_2(): lax.ppermute(head, axis, [((i + 1) % count, i) for i in range(ends)])  22.9 us
    reduce_sum x16, other arithmetic, count_block(): return jnp.sum(hits, axis=1)  22.6 us
    add x4, other arithmetic, transport(): result + weights[3] * window_at(0) + weights[4] * window_at(2 * MAPX)  17.8 us
    dynamic_update_slice x16, local copies, waits for them, and re-layouts, local(): counts = lax.map(count_block, local_cell).reshape(obs_count, row_count)  10.2 us
  transfers between devices with their start and end apart: 9, of which 6 were waited for; matrix products, arithmetic and copies ran while one was open for 8% of the time, Pallas kernels for 0%

profile of v1, /device:TPU:1, one launch (start us, length us, event | category | flops | bytes accessed | tf_op | source)
XLA Modules:
  0.0 429.1 jit_solution(9767882837820728476)
XLA Ops:
  6.5 2.0 copy.13
  9.6 5.6 %collective-permute-start = (f32[256,512]{0,1:T(8,128)}, f32[256,512]{0,1:T(8,128)}, u32[]{:S(2)}, u32[]{:S(2)}) collective-permute-start(f32[256,512]{0,1:T(8,128)} %get-tuple-element.48), channel_id=1, source_target_pairs={{0,32},{32,64},{64,96},{96,128},{128,160},{160,192},{192,224},{224... | collective-permute-start | bytes 1572872 | tf_op jit(solution)/shard_map/ppermute | solution.py:18
  17.7 5.3 %collective-permute-done = f32[256,512]{0,1:T(8,128)} collective-permute-done((f32[256,512]{0,1:T(8,128)}, f32[256,512]{0,1:T(8,128)}, u32[]{:S(2)}, u32[]{:S(2)}) %collective-permute-start) | collective-permute-done | bytes 524320 | tf_op jit(solution)/shard_map/ppermute | solution.py:18
  23.0 19.0 %collective-permute-done.1 = f32[256,512]{0,1:T(8,128)} collective-permute-done((f32[256,512]{0,1:T(8,128)}, f32[256,512]{0,1:T(8,128)}, u32[]{:S(2)}, u32[]{:S(2)}) %collective-permute-start.1) | collective-permute-done | bytes 524320 | tf_op jit(solution)/shard_map/ppermute | solution.py:20
  42.0 5.8 %fusion.14 = f32[1024,512]{0,1:T(8,128)S(1)} fusion(f32[1024,512]{0,1:T(8,128)} %copy-done.3, f32[256,512]{0,1:T(8,128)} %collective-permute-done.1, f32[256,512]{0,1:T(8,128)} %collective-permute-done, f32[1024]{0:T(1024)S(1)} %bitcast.38, f32[1024]{0:T(1024)S(1)} %bitcast.32, f32[1024]{0:T(1024)S(1)} %bitcast.34, f32[1024]{0:T(1024)S(1)} %bitcast.36, ...), kind=kLoop, calls=%fused_computation.33 | loop fusion | flops 6815744 | bytes 5263360 | tf_op jit(solution)/shard_map/add | solution.py:57
  47.8 1.5 fusion.44
  49.2 9.5 %collective-permute-start.2 = (f32[1024,256]{0,1:T(8,128)}, f32[1024,256]{0,1:T(8,128)}, u32[]{:S(2)}, u32[]{:S(2)}) collective-permute-start(f32[1024,256]{0,1:T(8,128)} %get-tuple-element.46), channel_id=1, source_target_pairs={{0,1},{1,2},{2,3},{3,4},{4,5},{5,6},{6,7},{7,8},{8,9},{9,10},{10,1... | collective-permute-start | bytes 3145736 | tf_op jit(solution)/shard_map/ppermute | solution.py:18
  58.7 1.9 collective-permute-start.3
  60.8 40.6 %collective-permute-done.2 = f32[1024,256]{0,1:T(8,128)} collective-permute-done((f32[1024,256]{0,1:T(8,128)}, f32[1024,256]{0,1:T(8,128)}, u32[]{:S(2)}, u32[]{:S(2)}) %collective-permute-start.2) | collective-permute-done | bytes 1048608 | tf_op jit(solution)/shard_map/ppermute | solution.py:18
  101.3 3.3 fusion.30
  106.0 22.3 %collective-permute-start.4 = (f32[256,512]{0,1:T(8,128)S(1)}, f32[256,512]{0,1:T(8,128)S(1)}, u32[]{:S(2)}, u32[]{:S(2)}) collective-permute-start(f32[256,512]{0,1:T(8,128)S(1)} %get-tuple-element.44), channel_id=1, source_target_pairs={{0,32},{32,64},{64,96},{96,128},{128,160},{160,192},{192,224},{224... | collective-permute-start | bytes 1572872 | tf_op jit(solution)/shard_map/ppermute | solution.py:18
  129.6 4.7 %collective-permute-done.4 = f32[256,512]{0,1:T(8,128)S(1)} collective-permute-done((f32[256,512]{0,1:T(8,128)S(1)}, f32[256,512]{0,1:T(8,128)S(1)}, u32[]{:S(2)}, u32[]{:S(2)}) %collective-permute-start.4) | collective-permute-done | bytes 524320 | tf_op jit(solution)/shard_map/ppermute | solution.py:18
  134.4 4.0 collective-permute-done.5
  138.3 5.4 %fusion.6 = f32[1024,512]{0,1:T(8,128)S(1)} fusion(f32[1024,512]{0,1:T(8,128)} %copy-done.4, f32[256,512]{0,1:T(8,128)} %collective-permute-done.5, f32[256,512]{0,1:T(8,128)S(1)} %collective-permute-done.4, f32[1024]{0:T(1024)S(1)} %bitcast.39, f32[1024]{0:T(1024)S(1)} %bitcast.33, f32[1024]{0:T(1024)S(1)} %bitcast.35, f32[1024]{0:T(1024)S(1)} %bitcast.37, ...), kind=kLoop, calls=%fused_computation.25 | loop fusion | flops 6815744 | bytes 5263360 | tf_op jit(solution)/shard_map/add | solution.py:57
  143.7 1.5 fusion.42
  145.2 9.8 %collective-permute-start.6 = (f32[1024,256]{0,1:T(8,128)}, f32[1024,256]{0,1:T(8,128)}, u32[]{:S(2)}, u32[]{:S(2)}) collective-permute-start(f32[1024,256]{0,1:T(8,128)} %get-tuple-element.42), channel_id=1, source_target_pairs={{0,1},{1,2},{2,3},{3,4},{4,5},{5,6},{6,7},{7,8},{8,9},{9,10},{10,1... | collective-permute-start | bytes 3145736 | tf_op jit(solution)/shard_map/ppermute | solution.py:18
  155.0 2.1 collective-permute-start.7
  157.1 33.0 %while.11 = (s32[]{:T(128)}, f32[16,16,1024]{2,1,0:T(8,128)}, s32[16,16,128]{2,1,0:T(8,128)S(1)}, s32[]{:T(128)}) while((s32[]{:T(128)}, f32[16,16,1024]{2,1,0:T(8,128)}, s32[16,16,128]{2,1,0:T(8,128)S(1)}, s32[]{:T(128)}) %tuple.42), condition=%wide.region_2.3_spmd.clone, body=%wide.region_0.2_spmd.clone.sunk | while | flops 6275074 | bytes 221253 | solution.py:83
  191.5 3.3 fusion.22
  196.1 2.8 fusion.46
  198.9 212.7 %all-gather.3.cloned.1.call-done = f32[4096,512]{1,0:T(8,128)} async-done(((f32[256,512]{1,0:T(8,128)}), f32[4096,512]{1,0:T(8,128)}) %all-gather.3.cloned.1.call-update) | async-done | bytes 8388624 | tf_op jit(solution)/shard_map/all_gather | solution.py:89
  411.6 4.5 %reduce_sum.18 = f32[256,512]{1,0:T(8,128)S(1)} reduce(f32[16,256,512]{2,1,0:T(8,128)} %bitcast.28, f32[]{:T(128)} %constant.63.clone.1), dimensions={0}, to_apply=%region_3.4 | reduce | flops 1966080 | bytes 8912900 | tf_op jit(solution)/shard_map/reduce_sum | solution.py:89
  416.2 3.2 bitcast_subtract_fusion
  419.4 2.9 copy.18
  (82 shorter events, 41.7 us)
Async XLA Ops:
  6.5 409.6 %copy-start = (bf16[1024,256]{1,0:T(8,128)(2,1)S(1)}, bf16[1024,256]{1,0:T(8,128)(2,1)}, u32[]{:S(2)}) copy-start(bf16[1024,256]{1,0:T(8,128)(2,1)} %param.13) | copy-start | bytes 1572868
  6.5 405.1 %all-gather.3.cloned.1.call-start = ((), (), s32[]{:S(2)}) async-start(), calls=%async_computation | async-start | bytes 8912896 | tf_op jit(solution)/shard_map/all_gather | solution.py:89
  8.5 33.4 %copy-start.3 = (f32[1024,512]{0,1:T(8,128)}, f32[1024,512]{0,1:T(8,128)S(1)}, u32[]{:S(2)}) copy-start(f32[1024,512]{0,1:T(8,128)S(1)} %copy.13) | copy-start | bytes 6291460
  8.5 8.0 %copy-start.6 = (s32[2,16384]{1,0:T(2,128)S(1)}, s32[2,16384]{1,0:T(2,128)}, u32[]{:S(2)}) copy-start(s32[2,16384]{1,0:T(2,128)} %param.9) | copy-start | bytes 393220
  8.5 8.0 %copy-start.7 = (f32[2,16384]{1,0:T(2,128)S(1)}, f32[2,16384]{1,0:T(2,128)}, u32[]{:S(2)}) copy-start(f32[2,16384]{1,0:T(2,128)} %param.10) | copy-start | bytes 393220
  9.6 13.4 %collective-permute-start = (f32[256,512]{0,1:T(8,128)}, f32[256,512]{0,1:T(8,128)}, u32[]{:S(2)}, u32[]{:S(2)}) collective-permute-start(f32[256,512]{0,1:T(8,128)} %get-tuple-element.48), channel_id=1, source_target_pairs={{0,32},{32,64},{64,96},{96,128},{128,160},{160,192},{192,224},{224... | collective-permute-start | bytes 1572872 | tf_op jit(solution)/shard_map/ppermute | solution.py:18
  15.3 26.7 %collective-permute-start.1 = (f32[256,512]{0,1:T(8,128)}, f32[256,512]{0,1:T(8,128)}, u32[]{:S(2)}, u32[]{:S(2)}) collective-permute-start(f32[256,512]{0,1:T(8,128)} %get-tuple-element.49), channel_id=1, source_target_pairs={{32,0},{64,32},{96,64},{128,96},{160,128},{192,160},{224,192},{256... | collective-permute-start | bytes 1572872 | tf_op jit(solution)/shard_map/ppermute | solution.py:20
  49.2 52.1 %collective-permute-start.2 = (f32[1024,256]{0,1:T(8,128)}, f32[1024,256]{0,1:T(8,128)}, u32[]{:S(2)}, u32[]{:S(2)}) collective-permute-start(f32[1024,256]{0,1:T(8,128)} %get-tuple-element.46), channel_id=1, source_target_pairs={{0,1},{1,2},{2,3},{3,4},{4,5},{5,6},{6,7},{7,8},{8,9},{9,10},{10,1... | collective-permute-start | bytes 3145736 | tf_op jit(solution)/shard_map/ppermute | solution.py:18
  58.7 42.6 %collective-permute-start.3 = (f32[1024,256]{0,1:T(8,128)}, f32[1024,256]{0,1:T(8,128)}, u32[]{:S(2)}, u32[]{:S(2)}) collective-permute-start(f32[1024,256]{0,1:T(8,128)} %get-tuple-element.47), channel_id=1, source_target_pairs={{1,0},{2,1},{3,2},{4,3},{5,4},{6,5},{7,6},{8,7},{9,8},{10,9},{11,1... | collective-permute-start | bytes 3145736 | tf_op jit(solution)/shard_map/ppermute | solution.py:20
  104.6 1.3 copy-start.4
  105.9 23.7 %copy-start.5 = (s32[256,128]{1,0:T(8,128)S(1)}, s32[256,128]{1,0:T(8,128)}, u32[]{:S(2)}) copy-start(s32[256,128]{1,0:T(8,128)} %param.11) | copy-start | bytes 393220
  106.0 28.4 %collective-permute-start.4 = (f32[256,512]{0,1:T(8,128)S(1)}, f32[256,512]{0,1:T(8,128)S(1)}, u32[]{:S(2)}, u32[]{:S(2)}) collective-permute-start(f32[256,512]{0,1:T(8,128)S(1)} %get-tuple-element.44), channel_id=1, source_target_pairs={{0,32},{32,64},{64,96},{96,128},{128,160},{160,192},{192,224},{224... | collective-permute-start | bytes 1572872 | tf_op jit(solution)/shard_map/ppermute | solution.py:18
  128.3 10.0 %collective-permute-start.5 = (f32[256,512]{0,1:T(8,128)S(1)}, f32[256,512]{0,1:T(8,128)}, u32[]{:S(2)}, u32[]{:S(2)}) collective-permute-start(f32[256,512]{0,1:T(8,128)S(1)} %get-tuple-element.45), channel_id=1, source_target_pairs={{32,0},{64,32},{96,64},{128,96},{160,128},{192,160},{224,192},{256... | collective-permute-start | bytes 1572872 | tf_op jit(solution)/shard_map/ppermute | solution.py:20
  143.7 46.4 %copy-start.8 = (f32[256]{0:T(256)S(1)}, f32[256]{0:T(256)}, u32[]{:S(2)}) copy-start(f32[256]{0:T(256)} %param.12) | copy-start | bytes 3076
  145.2 46.2 %collective-permute-start.6 = (f32[1024,256]{0,1:T(8,128)}, f32[1024,256]{0,1:T(8,128)}, u32[]{:S(2)}, u32[]{:S(2)}) collective-permute-start(f32[1024,256]{0,1:T(8,128)} %get-tuple-element.42), channel_id=1, source_target_pairs={{0,1},{1,2},{2,3},{3,4},{4,5},{5,6},{6,7},{7,8},{8,9},{9,10},{10,1... | collective-permute-start | bytes 3145736 | tf_op jit(solution)/shard_map/ppermute | solution.py:18
  155.0 36.5 %collective-permute-start.7 = (f32[1024,256]{0,1:T(8,128)}, f32[1024,256]{0,1:T(8,128)}, u32[]{:S(2)}, u32[]{:S(2)}) collective-permute-start(f32[1024,256]{0,1:T(8,128)} %get-tuple-element.43), channel_id=1, source_target_pairs={{1,0},{2,1},{3,2},{4,3},{5,4},{6,5},{7,6},{8,7},{9,8},{10,9},{11,1... | collective-permute-start | bytes 3145736 | tf_op jit(solution)/shard_map/ppermute | solution.py:20
  194.8 1.3 copy-start.1
  411.6 4.6 %copy-start.2 = (f32[1024,512]{0,1:T(8,128)S(1)}, f32[1024,512]{0,1:T(8,128)}, u32[]{:S(2)}) copy-start(f32[1024,512]{0,1:T(8,128)} %copy-done.1) | copy-start | bytes 6291460
Sparse Core Ops, SparseCore 0:
  199.0 212.5 all-gather.2
